TPU v7x, 32 devices: a whole 2x2x4 slice. The times are simulated.
32 devices in a mesh: px: 8 (over y, x, core), py: 4 (over z).
Axes of the slice: x: 2, y: 2, z: 4, core: 2. Of those that a mesh axis runs over, the one named last changes fastest.
Arguments:
- node_latents: bfloat16 [128, 80, 512], P('px', 'py'), may hold values from -6 to 6
- fine_edges: bfloat16 [128, 80, 6, 512], P('px', 'py'), may hold values from -6 to 6
- long_edges: bfloat16 [5120, 512], P(('px', 'py')), may hold values from -6 to 6
- neighbours: int32 [128, 80, 6], P('px', 'py'), may hold values from 0 to 7, as said below
- coarse_slots: int32 [640], P(('px', 'py')), may hold values from 0 to 319, as said below
- long_senders: int32 [5120], P(('px', 'py')), may hold values from 0 to 639
- long_receivers: int32 [5120], P(('px', 'py')), may hold values from 0 to 639, as said below
- edge_inner: bfloat16 [2, 1536, 512], replicated, may hold values from -0.15625 to 0.15625
- edge_outer: bfloat16 [2, 512, 512], replicated, may hold values from -0.25 to 0.25
- edge_gain: float32 [2, 512], replicated, may hold values from 0.5 to 1.5
- node_inner: bfloat16 [2, 1024, 512], replicated, may hold values from -0.1875 to 0.1875
- node_outer: bfloat16 [2, 512, 512], replicated, may hold values from -0.25 to 0.25
- node_gain: float32 [2, 512], replicated, may hold values from 0.5 to 1.5
Outputs:
- new_nodes: bfloat16 [128, 80, 512], P('px', 'py')
- new_fine: bfloat16 [128, 80, 6, 512], P('px', 'py')
- new_long: bfloat16 [5120, 512], P(('px', 'py'))
Inputs may be any that keep to these rules, and one draw needn't show every extreme that they name: `neighbours`: the 6 codes of one node are different. `coarse_slots`: the 20 entries of one device's block are different. `long_receivers`: among the 160 long edges of one device, at most 10 have receivers c with the same c // 20, and on every device some such group has exactly 10.
All inputs are finite; a program needn't handle non-finite values.
Results may differ from a plain program's by a relative error of at most 0.0095.
Values may be sent and summed in bfloat16 or wider, within the bound.
A program may use at most 128 MiB of HBM per device.

v0:
```python
import jax
import jax.numpy as jnp
from jax import lax
from jax.sharding import PartitionSpec as P

EPSILON = 1e-05


def with_halo(cells, sides, width):
    for axis, dim in sides:
        count = lax.axis_size(axis)
        head = lax.slice_in_dim(cells, 0, width, axis=dim)
        tail = lax.slice_in_dim(cells, cells.shape[dim] - width, cells.shape[dim], axis=dim)
        cells = jnp.concatenate(
            [
                lax.ppermute(tail, axis, [(i, (i + 1) % count) for i in range(count)]),
                cells,
                lax.ppermute(head, axis, [((i + 1) % count, i) for i in range(count)]),
            ],
            axis=dim,
        )
    return cells


def layer_norm(values, gains):
    center = values - jnp.mean(values, axis=-1, keepdims=True)
    spread = jnp.mean(center * center, axis=-1, keepdims=True)
    return center * lax.rsqrt(spread + EPSILON) * gains


def finish(before, inner_sum, outer, gains):
    hidden = jax.nn.silu(inner_sum).astype(jnp.bfloat16)
    output = jnp.dot(hidden, outer, preferred_element_type=jnp.float32)
    return (before.astype(jnp.float32) + layer_norm(output, gains)).astype(jnp.bfloat16)


def extended_index(neighbours, patch_columns):
    shifted_code = neighbours + (neighbours >= 4).astype(jnp.int32)
    rows_here = lax.broadcasted_iota(jnp.int32, neighbours.shape, 0)
    cols_here = lax.broadcasted_iota(jnp.int32, neighbours.shape, 1)
    row_step = shifted_code // 3 - 1
    column_step = shifted_code % 3 - 1
    return ((rows_here + 1 + row_step) * (patch_columns + 2) + cols_here + 1 + column_step).reshape(
        -1
    )


def owner_sums(receivers, messages, coarse_count, devices):
    long_count, features = messages.shape
    capacity = (2 * long_count + devices - 1) // devices
    owners = receivers // coarse_count
    matches = (owners[:, None] == lax.iota(jnp.int32, devices)[None, :]).astype(jnp.int32)
    before = jnp.cumsum(matches, axis=0) - matches
    ranking = jnp.sum(before * matches, axis=1)
    placed = owners * capacity + ranking
    bucket = jnp.zeros((devices * capacity, features), jnp.bfloat16).at[placed].set(messages)
    labels = (
        jnp.full((devices * capacity,), coarse_count, jnp.int32)
        .at[placed]
        .set(receivers % coarse_count)
    )
    arrived, arrived_tags = (
        lax.all_to_all(
            bucket.reshape(devices, capacity, features),
            ("px", "py"),
            split_axis=0,
            concat_axis=0,
            tiled=True,
        ),
        lax.all_to_all(
            labels.astype(jnp.bfloat16).reshape(devices, capacity),
            ("px", "py"),
            split_axis=0,
            concat_axis=0,
            tiled=True,
        ),
    )
    tag_values = arrived_tags.reshape(-1).astype(jnp.int32)
    chooser = (tag_values[:, None] == lax.iota(jnp.int32, coarse_count)[None, :]).astype(
        jnp.bfloat16
    )
    return lax.dot_general(
        chooser,
        arrived.reshape(-1, features),
        (((0,), (0,)), ((), ())),
        preferred_element_type=jnp.float32,
    )


def shards(
    node_latents,
    fine_edges,
    long_edges,
    neighbours,
    coarse_slots,
    long_senders,
    long_receivers,
    edge_inner,
    edge_outer,
    edge_gain,
    node_inner,
    node_outer,
    node_gain,
):
    patch_rows, patch_columns, features = node_latents.shape
    degree = fine_edges.shape[2]
    coarse_count = coarse_slots.shape[0]
    layers = edge_inner.shape[0]
    devices = lax.axis_size("px") * lax.axis_size("py")
    patch_cells = patch_rows * patch_columns
    sender_index = extended_index(neighbours, patch_columns)
    latents = node_latents.reshape(patch_cells, features)
    fine_rows = fine_edges.reshape(patch_cells * degree, features)
    long_rows = long_edges
    for layer_index in range(layers):
        edge_part = edge_inner[layer_index, :features]
        send_part = edge_inner[layer_index, features : 2 * features]
        receive_part = edge_inner[layer_index, 2 * features :]
        own_coarse = jnp.take(latents, coarse_slots, axis=0)
        coarse = lax.all_gather(own_coarse, ("px", "py"), axis=0, tiled=True)
        padded = with_halo(
            latents.reshape(patch_rows, patch_columns, features), (("px", 0), ("py", 1)), 1
        )
        sender_terms = jnp.dot(
            padded.reshape(-1, features), send_part, preferred_element_type=jnp.float32
        )
        receiver_terms = jnp.dot(latents, receive_part, preferred_element_type=jnp.float32)
        inner_sum = jnp.dot(fine_rows, edge_part, preferred_element_type=jnp.float32) + jnp.take(
            sender_terms, sender_index, axis=0
        )
        inner_sum = (
            inner_sum.reshape(patch_cells, degree, -1) + receiver_terms[:, None, :]
        ).reshape(patch_cells * degree, -1)
        fine_rows = finish(fine_rows, inner_sum, edge_outer[layer_index], edge_gain[layer_index])
        long_sum = jnp.dot(long_rows, edge_part, preferred_element_type=jnp.float32)
        long_sum = long_sum + jnp.dot(
            jnp.take(coarse, long_senders, axis=0), send_part, preferred_element_type=jnp.float32
        )
        long_sum = long_sum + jnp.dot(
            jnp.take(coarse, long_receivers, axis=0),
            receive_part,
            preferred_element_type=jnp.float32,
        )
        long_rows = finish(long_rows, long_sum, edge_outer[layer_index], edge_gain[layer_index])
        coarse_sum = owner_sums(long_receivers, long_rows, coarse_count, devices)
        incoming = jnp.sum(
            fine_rows.reshape(patch_cells, degree, features), axis=1, dtype=jnp.float32
        )
        incoming = incoming.at[coarse_slots].add(coarse_sum).astype(jnp.bfloat16)
        node_sum = jnp.dot(
            latents, node_inner[layer_index, :features], preferred_element_type=jnp.float32
        )
        node_sum = node_sum + jnp.dot(
            incoming, node_inner[layer_index, features:], preferred_element_type=jnp.float32
        )
        latents = finish(latents, node_sum, node_outer[layer_index], node_gain[layer_index])
    return (
        latents.reshape(patch_rows, patch_columns, features),
        fine_rows.reshape(fine_edges.shape),
        long_rows,
    )


def solution(mesh):
    in_specs = (
        P("px", "py", None),
        P("px", "py", None, None),
        P(("px", "py"), None),
        P("px", "py", None),
        P(("px", "py")),
        P(("px", "py")),
        P(("px", "py")),
        P(),
        P(),
        P(),
        P(),
        P(),
        P(),
    )
    out_specs = (P("px", "py", None), P("px", "py", None, None), P(("px", "py"), None))
    return jax.shard_map(shards, mesh=mesh, in_specs=in_specs, out_specs=out_specs, check_vma=False)
```

profile of v0, /device:TPU:0, one launch (start us, length us, event | category | flops | bytes accessed | tf_op | source)
XLA Modules:
  0.0 335.7 jit_solution(288377839166334916)
XLA Ops:
  0.7 1.7 fusion.139
  2.4 3.4 %collective-permute-start.1 = (bf16[1,20,512]{2,0,1:T(2,128)(2,1)}, bf16[1,20,512]{2,0,1:T(2,128)(2,1)S(1)}, u32[]{:S(2)}, u32[]{:S(2)}) collective-permute-start(bf16[1,20,512]{2,0,1:T(2,128)(2,1)} %get-tuple-element.22), channel_id=1, source_target_pairs={{4,0},{8,4},{12,8},{16,12},{20,16},{24,20},{28,24},{0,28},{5,1},{9... | collective-permute-start | bytes 61448 | tf_op jit(solution)/shard_map/ppermute | solution.py:18
  9.3 6.0 %all-to-all-start = ((bf16[32,1,10]{2,1,0:T(2,128)(2,1)}), bf16[32,1,10]{2,1,0:T(2,128)(2,1)S(1)}, u32[]{:S(2)}, u32[]{:S(2)}) async-start(bf16[32,1,10]{2,1,0:T(2,128)(2,1)} %all_to_all.17), calls=%async_computation | async-start | bytes 32768 | tf_op jit(solution)/shard_map/all_to_all | solution.py:70
  21.8 2.2 fusion.42
  24.0 2.2 fusion.33
  28.8 75.4 %all-gather = bf16[32,20,512]{2,1,0:T(8,128)(2,1)S(1)} all-gather(bf16[1,20,512]{2,1,0:T(8,128)(2,1)S(1)} %select_bitcast_fusion.1), channel_id=1, replica_groups=mesh['px'=8,'py'=4] {'px','py'}, dimensions={0}, use_global_device_ids=true | all-gather | bytes 675840 | tf_op jit(solution)/shard_map/all_gather | solution.py:120
  107.6 1.8 fusion.145
  110.5 2.1 fusion.20
  112.5 2.7 copy.29
  115.2 2.1 reshape.173
  117.3 4.1 %add.211 = f32[320,6,512]{2,1,0:T(8,128)} broadcast(f32[320,512]{1,0:T(8,128)} %fusion.33), dimensions={0,2} | broadcast | bytes 4587520 | tf_op jit(solution)/shard_map/add | solution.py:132
  121.4 5.6 %add.212 = f32[1920,512]{1,0:T(8,128)} reshape(f32[320,6,512]{2,1,0:T(8,128)} %add.211) | data formatting | bytes 7864320 | tf_op jit(solution)/shard_map/add | solution.py:132
  129.4 2.0 collective-permute-start.2
  131.5 3.5 %all-to-all-start.1 = ((bf16[32,10,512]{2,1,0:T(8,128)(2,1)}), bf16[32,10,512]{2,1,0:T(8,128)(2,1)}, u32[]{:S(2)}, u32[]{:S(2)}) async-start(bf16[32,10,512]{2,1,0:T(8,128)(2,1)} %reshape.178), calls=%async_computation.1 | async-start | bytes 1048576 | tf_op jit(solution)/shard_map/all_to_all | solution.py:63
  135.7 1.4 fusion.36
  137.2 6.2 %gather_fusion = f32[1920,512]{1,0:T(8,128)} fusion(f32[396,512]{1,0:T(8,128)S(1)} %fusion.36, s32[2048]{0:T(1024)S(1)} %pad_clamp_fusion), kind=kCustom, calls=%fused_computation.clone | custom fusion | bytes 7872000 | tf_op jit(solution)/shard_map/jit(_take)/gather | solution.py:128
  143.3 8.2 %fusion.142 = (f32[1920]{0:T(1024)S(1)}, f32[1920,512]{1,0:T(8,128)}) fusion(bf16[2,512,512]{2,1,0:T(8,128)(2,1)} %param.27, f32[1920,512]{1,0:T(8,128)} %add.212, f32[1920,512]{1,0:T(8,128)} %gather_fusion, bf16[1920,512]{1,0:T(8,128)(2,1)S(1)} %copy-done.4, pred[1920]{0:T(1024)(128)(4,1)S(1)} %copy-done.32, bf16[2,1536,512]{2,1,0:T(8,128)(2,1)} %param.26), kind=kOutput, calls=%fused_computation.210 | convolution fusion | flops 2022111360 | bytes 14820736 | tf_op jit(solution)/shard_map/dot_general | solution.py:33
  151.6 2.9 multiply_reduce_fusion.1
  154.9 2.5 add_convert_fusion.1
  157.3 2.9 reshape.186
  160.3 5.0 %reduce_sum.141 = f32[320,512]{1,0:T(8,128)} reduce(f32[320,6,512]{2,1,0:T(8,128)} %reshape.186, f32[]{:T(128)} %constant.121.clone.1), dimensions={1}, to_apply=%region_2.4 | reduce | flops 819200 | bytes 4587524 | tf_op jit(solution)/shard_map/reduce_sum | solution.py:146
  166.7 2.6 scatter_fusion
  169.3 2.3 fusion.150
  172.1 2.3 fusion.24
  174.4 2.2 fusion.15
  178.0 79.7 %all-gather.1 = bf16[32,20,512]{2,1,0:T(8,128)(2,1)} all-gather(bf16[1,20,512]{2,1,0:T(8,128)(2,1)S(1)} %select_bitcast_fusion), channel_id=1, replica_groups=mesh['px'=8,'py'=4] {'px','py'}, dimensions={0}, use_global_device_ids=true | all-gather | bytes 675840 | tf_op jit(solution)/shard_map/all_gather | solution.py:120
  259.0 1.7 gather_fusion.6
  260.8 1.6 gather_fusion.7
  262.4 2.6 collective-permute-start.5
  265.0 2.2 convolution_add_fusion.3
  267.2 2.0 fusion.158
  272.1 2.0 collective-permute-start.6
  274.1 1.8 add_convert_fusion.4
  275.9 3.1 add.231
  279.0 5.6 %add.232 = f32[1920,512]{1,0:T(8,128)} reshape(f32[320,6,512]{2,1,0:T(8,128)} %add.231) | data formatting | bytes 7864320 | tf_op jit(solution)/shard_map/add | solution.py:132
  284.6 1.6 scatter_custom_fusion.3
  287.2 3.3 all-to-all-start.2
  291.7 1.4 fusion.18
  293.1 6.5 %gather_fusion.4 = f32[1920,512]{1,0:T(8,128)} fusion(f32[396,512]{1,0:T(8,128)S(1)} %fusion.18, s32[2048]{0:T(1024)} %copy-done.14), kind=kCustom, calls=%fused_computation.3.clone | custom fusion | bytes 7872000 | tf_op jit(solution)/shard_map/jit(_take)/gather | solution.py:128
  299.6 8.3 %fusion.155 = (f32[1920]{0:T(1024)S(1)}, f32[1920,512]{1,0:T(8,128)}) fusion(bf16[2,512,512]{2,1,0:T(8,128)(2,1)} %param.27, f32[1920,512]{1,0:T(8,128)} %add.232, f32[1920,512]{1,0:T(8,128)} %gather_fusion.4, pred[1920]{0:T(1024)(128)(4,1)S(1)} %copy-done.33, bf16[1920,512]{1,0:T(8,128)(2,1)S(1)} %add_convert_fusion.1, bf16[2,1536,512]{2,1,0:T(8,128)(2,1)} %param.26), kind=kOutput, calls=%fused_computation.213 | convolution fusion | flops 2022111360 | bytes 14820736 | tf_op jit(solution)/shard_map/dot_general | solution.py:33
  307.9 2.9 multiply_reduce_fusion
  311.2 2.2 add_convert_fusion
  313.4 4.7 %reshape.189 = f32[320,6,512]{2,1,0:T(8,128)} reshape(bf16[1920,512]{1,0:T(8,128)(2,1)} %add_convert_fusion) | data formatting | bytes 5898240 | tf_op jit(solution)/shard_map/convert_element_type | solution.py:146
  318.1 2.3 reshape.185
  320.4 5.1 %reduce_sum.149 = f32[320,512]{1,0:T(8,128)} reduce(f32[320,6,512]{2,1,0:T(8,128)} %reshape.189, f32[]{:T(128)} %constant.121.clone.1), dimensions={1}, to_apply=%region_15.19 | reduce | flops 819200 | bytes 4587524 | tf_op jit(solution)/shard_map/reduce_sum | solution.py:146
  325.5 2.4 copy.36
  329.4 2.6 scatter_fusion.1
  332.0 2.3 fusion.163
  (172 shorter events, 32.9 us)
Async XLA Ops:
  0.6 25.6 %copy-start.26 = (f32[2,512]{1,0:T(2,128)S(1)}, f32[2,512]{1,0:T(2,128)}, u32[]{:S(2)}) copy-start(f32[2,512]{1,0:T(2,128)} %param.28) | copy-start | bytes 12292
  0.6 26.1 %copy-start.13 = (bf16[160,512]{1,0:T(8,128)(2,1)S(1)}, bf16[160,512]{1,0:T(8,128)(2,1)}, u32[]{:S(2)}) copy-start(bf16[160,512]{1,0:T(8,128)(2,1)} %param.21) | copy-start | bytes 491524
  2.4 127.0 %collective-permute-start.1 = (bf16[1,20,512]{2,0,1:T(2,128)(2,1)}, bf16[1,20,512]{2,0,1:T(2,128)(2,1)S(1)}, u32[]{:S(2)}, u32[]{:S(2)}) collective-permute-start(bf16[1,20,512]{2,0,1:T(2,128)(2,1)} %get-tuple-element.22), channel_id=1, source_target_pairs={{4,0},{8,4},{12,8},{16,12},{20,16},{24,20},{28,24},{0,28},{5,1},{9... | collective-permute-start | bytes 61448 | tf_op jit(solution)/shard_map/ppermute | solution.py:18
  5.7 123.6 %collective-permute-start = (bf16[1,20,512]{2,0,1:T(2,128)(2,1)}, bf16[1,20,512]{2,0,1:T(2,128)(2,1)S(1)}, u32[]{:S(2)}, u32[]{:S(2)}) collective-permute-start(bf16[1,20,512]{2,0,1:T(2,128)(2,1)} %get-tuple-element.21), channel_id=1, source_target_pairs={{0,4},{4,8},{8,12},{12,16},{16,20},{20,24},{24,28},{28,0},{1,5},{5... | collective-permute-start | bytes 61448 | tf_op jit(solution)/shard_map/ppermute | solution.py:16
  7.4 20.7 %copy-start.34 = (s32[160]{0:T(256)}, s32[160]{0:T(256)S(1)}, u32[]{:S(2)}) copy-start(s32[160]{0:T(256)S(1)} %compare_select_fusion.3) | copy-start | bytes 1924
  9.3 122.2 %all-to-all-start = ((bf16[32,1,10]{2,1,0:T(2,128)(2,1)}), bf16[32,1,10]{2,1,0:T(2,128)(2,1)S(1)}, u32[]{:S(2)}, u32[]{:S(2)}) async-start(bf16[32,1,10]{2,1,0:T(2,128)(2,1)} %all_to_all.17), calls=%async_computation | async-start | bytes 32768 | tf_op jit(solution)/shard_map/all_to_all | solution.py:70
  19.0 86.4 %copy-start.23 = (s32[20]{0:T(128)}, s32[20]{0:T(128)S(1)}, u32[]{:S(2)}) copy-start(s32[20]{0:T(128)S(1)} %compare_select_fusion.4) | copy-start | bytes 244
  19.6 9.2 %copy-start.30 = (pred[20]{0:T(512)(128)(4,1)}, pred[20]{0:T(512)(128)(4,1)S(1)}, u32[]{:S(2)}) copy-start(pred[20]{0:T(512)(128)(4,1)S(1)} %compare_and_fusion.3) | copy-start | bytes 64
  21.0 85.3 %copy-start.28 = (pred[160]{0:T(512)(128)(4,1)}, pred[160]{0:T(512)(128)(4,1)S(1)}, u32[]{:S(2)}) copy-start(pred[160]{0:T(512)(128)(4,1)S(1)} %compare_and_fusion.2) | copy-start | bytes 484
  21.7 85.9 %copy-start.35 = (pred[160]{0:T(512)(128)(4,1)}, pred[160]{0:T(512)(128)(4,1)S(1)}, u32[]{:S(2)}) copy-start(pred[160]{0:T(512)(128)(4,1)S(1)} %compare_and_fusion.1) | copy-start | bytes 484
  28.1 76.2 %copy-start.22 = (s32[1024]{0:T(1024)}, s32[1024]{0:T(1024)S(1)}, u32[]{:S(2)}) copy-start(s32[1024]{0:T(1024)S(1)} %pad_clamp_fusion.3) | copy-start | bytes 12292
  104.4 5.1 %copy-start.19 = (s32[1024]{0:T(1024)}, s32[1024]{0:T(1024)S(1)}, u32[]{:S(2)}) copy-start(s32[1024]{0:T(1024)S(1)} %get-tuple-element.43) | copy-start | bytes 12292
  104.4 5.3 %copy-start.27 = (f32[2,512]{1,0:T(2,128)S(1)}, f32[2,512]{1,0:T(2,128)}, u32[]{:S(2)}) copy-start(f32[2,512]{1,0:T(2,128)} %param.31) | copy-start | bytes 12292
  110.4 16.6 %copy-start.7 = (bf16[160,512]{1,0:T(8,128)(2,1)}, bf16[160,512]{1,0:T(8,128)(2,1)S(1)}, u32[]{:S(2)}) copy-start(bf16[160,512]{1,0:T(8,128)(2,1)S(1)} %add_convert_fusion.5) | copy-start | bytes 491524
  112.5 24.6 %copy-start.14 = (s32[2048]{0:T(1024)}, s32[2048]{0:T(1024)S(1)}, u32[]{:S(2)}) copy-start(s32[2048]{0:T(1024)S(1)} %pad_clamp_fusion) | copy-start | bytes 24580
  121.4 7.9 %copy-start.5 = (bf16[16,20,512]{2,0,1:T(8,128)(2,1)S(1)}, bf16[16,20,512]{2,0,1:T(8,128)(2,1)}, u32[]{:S(2)}) copy-start(bf16[16,20,512]{2,0,1:T(8,128)(2,1)} %param.19) | copy-start | bytes 983044
  129.4 5.8 %collective-permute-start.3 = (bf16[18,1,512]{2,0,1:T(8,128)(2,1)S(1)}, bf16[18,1,512]{2,0,1:T(8,128)(2,1)S(1)}, u32[]{:S(2)}, u32[]{:S(2)}) collective-permute-start(bf16[18,1,512]{2,0,1:T(8,128)(2,1)S(1)} %get-tuple-element.18), channel_id=1, source_target_pairs={{1,0},{2,1},{3,2},{0,3},{5,4},{6,5},{7,6},{4,7},{9,8},{10,9},{11,1... | collective-permute-start | bytes 55304 | tf_op jit(solution)/shard_map/ppermute | solution.py:18
  129.4 5.7 %collective-permute-start.2 = (bf16[18,1,512]{2,0,1:T(8,128)(2,1)S(1)}, bf16[18,1,512]{2,0,1:T(8,128)(2,1)S(1)}, u32[]{:S(2)}, u32[]{:S(2)}) collective-permute-start(bf16[18,1,512]{2,0,1:T(8,128)(2,1)S(1)} %get-tuple-element.17), channel_id=1, source_target_pairs={{0,1},{1,2},{2,3},{3,0},{4,5},{5,6},{6,7},{7,4},{8,9},{9,10},{10,1... | collective-permute-start | bytes 55304 | tf_op jit(solution)/shard_map/ppermute | solution.py:16
  131.5 33.8 %all-to-all-start.1 = ((bf16[32,10,512]{2,1,0:T(8,128)(2,1)}), bf16[32,10,512]{2,1,0:T(8,128)(2,1)}, u32[]{:S(2)}, u32[]{:S(2)}) async-start(bf16[32,10,512]{2,1,0:T(8,128)(2,1)} %reshape.178), calls=%async_computation.1 | async-start | bytes 1048576 | tf_op jit(solution)/shard_map/all_to_all | solution.py:63
  135.2 31.2 %copy-start.15 = (s32[320]{0:T(512)}, s32[320]{0:T(512)S(1)}, u32[]{:S(2)}) copy-start(s32[320]{0:T(512)S(1)} %reshape.188) | copy-start | bytes 3844
  137.1 6.2 %copy-start.4 = (bf16[1920,512]{1,0:T(8,128)(2,1)S(1)}, bf16[1920,512]{1,0:T(8,128)(2,1)}, u32[]{:S(2)}) copy-start(bf16[1920,512]{1,0:T(8,128)(2,1)} %reshape.173) | copy-start | bytes 5898244
  137.2 6.2 %copy-start.32 = (pred[1920]{0:T(1024)(128)(4,1)S(1)}, pred[1920]{0:T(1024)(128)(4,1)}, u32[]{:S(2)}) copy-start(pred[1920]{0:T(1024)(128)(4,1)} %compare_and_fusion) | copy-start | bytes 5764
  151.6 3.3 copy-start.2
  160.3 6.4 %copy-start.24 = (s32[20]{0:T(128)S(1)}, s32[20]{0:T(128)}, u32[]{:S(2)}) copy-start(s32[20]{0:T(128)} %copy-done.23) | copy-start | bytes 244
  165.2 6.7 %copy-start.21 = (f32[1,512]{1,0:T(1,128)S(1)}, f32[1,512]{1,0:T(1,128)}, u32[]{:S(2)}) copy-start(f32[1,512]{1,0:T(1,128)} %get-tuple-element.24) | copy-start | bytes 6148
  171.6 6.3 %copy-start.31 = (pred[20]{0:T(512)(128)(4,1)S(1)}, pred[20]{0:T(512)(128)(4,1)}, u32[]{:S(2)}) copy-start(pred[20]{0:T(512)(128)(4,1)} %copy-done.30) | copy-start | bytes 64
  172.1 92.9 %copy-start.10 = (f32[160,512]{1,0:T(8,128)S(1)}, f32[160,512]{1,0:T(8,128)}, u32[]{:S(2)}) copy-start(f32[160,512]{1,0:T(8,128)} %fusion.20) | copy-start | bytes 983044
  172.1 92.9 %copy-start.29 = (pred[160]{0:T(512)(128)(4,1)S(1)}, pred[160]{0:T(512)(128)(4,1)}, u32[]{:S(2)}) copy-start(pred[160]{0:T(512)(128)(4,1)} %copy-done.28) | copy-start | bytes 484
  174.4 92.8 %copy-start.36 = (pred[160]{0:T(512)(128)(4,1)S(1)}, pred[160]{0:T(512)(128)(4,1)}, u32[]{:S(2)}) copy-start(pred[160]{0:T(512)(128)(4,1)} %copy-done.35) | copy-start | bytes 484
  260.8 13.3 %copy-start.8 = (bf16[160,512]{1,0:T(8,128)(2,1)S(1)}, bf16[160,512]{1,0:T(8,128)(2,1)}, u32[]{:S(2)}) copy-start(bf16[160,512]{1,0:T(8,128)(2,1)} %copy-done.7) | copy-start | bytes 491524
  262.3 13.5 %copy-start.6 = (f32[320,512]{1,0:T(8,128)S(1)}, f32[320,512]{1,0:T(8,128)}, u32[]{:S(2)}) copy-start(f32[320,512]{1,0:T(8,128)} %fusion.15) | copy-start | bytes 1966084
  262.3 8.2 %collective-permute-start.4 = (bf16[1,20,512]{2,1,0:T(8,128)(2,1)}, bf16[1,20,512]{2,1,0:T(8,128)(2,1)S(1)}, u32[]{:S(2)}, u32[]{:S(2)}) collective-permute-start(bf16[1,20,512]{2,1,0:T(8,128)(2,1)} %get-tuple-element.20), channel_id=1, source_target_pairs={{0,4},{4,8},{8,12},{12,16},{16,20},{20,24},{24,28},{28,0},{1,5},{5... | collective-permute-start | bytes 61448 | tf_op jit(solution)/shard_map/ppermute | solution.py:16
  262.4 8.2 %collective-permute-start.5 = (bf16[1,20,512]{2,1,0:T(8,128)(2,1)}, bf16[1,20,512]{2,1,0:T(8,128)(2,1)S(1)}, u32[]{:S(2)}, u32[]{:S(2)}) collective-permute-start(bf16[1,20,512]{2,1,0:T(8,128)(2,1)} %get-tuple-element.19), channel_id=1, source_target_pairs={{4,0},{8,4},{12,8},{16,12},{20,16},{24,20},{28,24},{0,28},{5,1},{9... | collective-permute-start | bytes 61448 | tf_op jit(solution)/shard_map/ppermute | solution.py:18
  269.1 0.7 copy-start.9
  269.2 0.7 copy-start.18
  270.6 0.8 copy-start.11
  272.1 18.4 %collective-permute-start.7 = (bf16[18,1,512]{2,1,0:T(2,128)(2,1)}, bf16[18,1,512]{2,1,0:T(2,128)(2,1)}, u32[]{:S(2)}, u32[]{:S(2)}) collective-permute-start(bf16[18,1,512]{2,1,0:T(2,128)(2,1)} %get-tuple-element.16), channel_id=1, source_target_pairs={{1,0},{2,1},{3,2},{0,3},{5,4},{6,5},{7,6},{4,7},{9,8},{10,9},{11,1... | collective-permute-start | bytes 55304 | tf_op jit(solution)/shard_map/ppermute | solution.py:18
  272.1 18.4 %collective-permute-start.6 = (bf16[18,1,512]{2,1,0:T(2,128)(2,1)}, bf16[18,1,512]{2,1,0:T(2,128)(2,1)}, u32[]{:S(2)}, u32[]{:S(2)}) collective-permute-start(bf16[18,1,512]{2,1,0:T(2,128)(2,1)} %get-tuple-element.15), channel_id=1, source_target_pairs={{0,1},{1,2},{2,3},{3,0},{4,5},{5,6},{6,7},{7,4},{8,9},{9,10},{10,1... | collective-permute-start | bytes 55304 | tf_op jit(solution)/shard_map/ppermute | solution.py:16
  279.0 11.5 %copy-start.12 = (bf16[18,20,512]{2,1,0:T(8,128)(2,1)S(1)}, bf16[18,20,512]{2,1,0:T(8,128)(2,1)}, u32[]{:S(2)}) copy-start(bf16[18,20,512]{2,1,0:T(8,128)(2,1)} %copy-done.11) | copy-start | bytes 1105924
  287.2 40.7 %all-to-all-start.2 = ((bf16[32,10,512]{2,1,0:T(8,128)(2,1)}), bf16[32,10,512]{2,1,0:T(8,128)(2,1)}, u32[]{:S(2)}, u32[]{:S(2)}) async-start(bf16[32,10,512]{2,1,0:T(8,128)(2,1)} %reshape.182), calls=%async_computation.2 | async-start | bytes 1048576 | tf_op jit(solution)/shard_map/all_to_all | solution.py:63
  293.1 6.5 %copy-start.33 = (pred[1920]{0:T(1024)(128)(4,1)S(1)}, pred[1920]{0:T(1024)(128)(4,1)}, u32[]{:S(2)}) copy-start(pred[1920]{0:T(1024)(128)(4,1)} %compare_and_fusion) | copy-start | bytes 5764
  307.9 3.3 copy-start.1
  307.9 3.3 copy-start.17
  313.4 4.7 %copy-start = (bf16[1920,512]{1,0:T(8,128)(2,1)S(1)}, bf16[1920,512]{1,0:T(8,128)(2,1)}, u32[]{:S(2)}) copy-start(bf16[1920,512]{1,0:T(8,128)(2,1)} %add_convert_fusion) | copy-start | bytes 5898244
  320.4 5.1 %copy-start.3 = (bf16[16,20,6,512]{3,2,1,0:T(8,128)(2,1)S(1)}, bf16[16,20,6,512]{3,2,1,0:T(8,128)(2,1)}, u32[]{:S(2)}) copy-start(bf16[16,20,6,512]{3,2,1,0:T(8,128)(2,1)} %reshape.185) | copy-start | bytes 5898244
  325.5 3.5 %copy-start.16 = (s32[320]{0:T(512)S(1)}, s32[320]{0:T(512)}, u32[]{:S(2)}) copy-start(s32[320]{0:T(512)} %copy-done.15) | copy-start | bytes 3844
  325.5 3.8 %copy-start.25 = (s32[20]{0:T(128)S(1)}, s32[20]{0:T(128)}, u32[]{:S(2)}) copy-start(s32[20]{0:T(128)} %copy-done.23) | copy-start | bytes 244
  327.9 6.7 %copy-start.20 = (f32[1,512]{1,0:T(1,128)S(1)}, f32[1,512]{1,0:T(1,128)}, u32[]{:S(2)}) copy-start(f32[1,512]{1,0:T(1,128)} %get-tuple-element.23) | copy-start | bytes 6148
where the time goes:
time: 338 us; the launch traced here: 336 us
  blocking collectives  155 us (46%)
  local copies, waits for them, and re-layouts  74.5 us (22%)
  matrix products  44.2 us (13%)
  other arithmetic  37.5 us (11%)
  starting transfers between devices  23 us (7%)
    all_gather x2, blocking collectives, shards(): coarse = lax.all_gather(own_coarse, ('px', 'py'), axis=0, tiled=True)  155 us
    dot_general x6, matrix products, finish(): output = jnp.dot(hidden, outer, preferred_element_type=jnp.float32)  25 us
    add x4, local copies, waits for them, and re-layouts, shards(): inner_sum.reshape(patch_cells, degree, -1) + receiver_terms[:, None, :]  18.4 us
    gather x2, local copies, waits for them, and re-layouts, shards(): jnp.take(sender_terms, sender_index, axis=0)  12.6 us
    unnamed x82, local copies, waits for them, and re-layouts  10.5 us
    reduce_sum x2, other arithmetic, shards(): jnp.sum(fine_rows.reshape(patch_cells, degree, features), axis=1, dtype=j...  10.1 us
    convert_element_type x2, local copies, waits for them, and re-layouts, shards(): jnp.sum(fine_rows.reshape(patch_cells, degree, features), axis=1, dtype=j...  7.58 us
    convert_element_type x6, other arithmetic, finish(): (before.astype(jnp.float32) + layer_norm(output, gains)).astype(jnp.bfloa...  7 us
  transfers between devices with their start and end apart: 11, of which 0 were waited for; matrix products, arithmetic and copies ran while one was open for 38% of the time, Pallas kernels for 0%

commit v1 on v0

v1 whole, which is shorter than its diff:
```python
import functools

import jax
import jax.numpy as jnp
import numpy as np
from jax import lax
from jax.experimental import pallas as pl
from jax.experimental.pallas import tpu as pltpu
from jax.sharding import PartitionSpec as P

EPSILON = 1e-05
MESH = pl.DeviceIdType.MESH
BF = jnp.bfloat16
F32 = jnp.float32


def up16(count):
    return -(-count // 16) * 16


def dot(a, b):
    return jnp.dot(a, b, preferred_element_type=F32)


def onehot(index, shape, axis):
    return jnp.where(lax.broadcasted_iota(jnp.int32, shape, axis) == index, 1.0, 0.0).astype(BF)


def finish(before, inner_sum, outer, gains):
    hidden = (0.5 * inner_sum * (1.0 + jnp.tanh(0.5 * inner_sum))).astype(BF)
    output = dot(hidden, outer)
    center = output - jnp.mean(output, axis=-1, keepdims=True)
    spread = jnp.mean(center * center, axis=-1, keepdims=True)
    return (before.astype(F32) + center * lax.rsqrt(spread + EPSILON) * gains).astype(BF)


def kernel(
    rows, columns, counts, block,
    lat_ref, fine_ref, long_ref, sidx_ref, pidx_ref, cols_ref, place_ref, slots_ref,
    eg_ref, ng_ref, ei_hbm, eo_hbm, ni_hbm, no_hbm,
    nodes_out, fine_out, long_out,
    h_ref, onehots, spread_ref, recv_terms, incoming, select_ref,
    send_buf, source, coarse, bucket, arrived, labels_out, labels_in,
    ei, eo, ni, no,
    w_sem, halo_send, halo_recv, coarse_send, coarse_recv,
    bucket_send, bucket_recv, label_send, label_recv,
):
    npx, npy = counts
    devices = npx * npy
    cells, features = lat_ref.shape
    degree = fine_ref.shape[1]
    layers = ei.shape[0]
    cslots = up16(slots_ref.shape[1])
    x, y = lax.axis_index("px"), lax.axis_index("py")
    me = x * npy + y
    down, up = lax.rem(x + 1, npx), lax.rem(x + npx - 1, npx)
    right, left = lax.rem(y + 1, npy), lax.rem(y + npy - 1, npy)
    wr, hr = up16(columns), up16(rows)
    sizes = (wr, wr, hr, hr, 16, 16, 16, 16)
    offsets = tuple(int(v) for v in np.cumsum((0,) + sizes))
    halo = offsets[-1]
    targets = (
        (down, y), (up, y), (x, right), (x, left),
        (down, right), (down, left), (up, right), (up, left),
    )

    loads = []
    for layer in range(layers):
        for j, (src, dst) in enumerate(((ei_hbm, ei), (eo_hbm, eo), (ni_hbm, ni), (no_hbm, no))):
            copy = pltpu.make_async_copy(src.at[layer], dst.at[layer], w_sem.at[layer, j])
            copy.start()
            loads.append(copy)

    def place(base, size):
        return pl.ds(pl.multiple_of(base * size, size), size)

    def to_all(src_of, dst, send_sem, recv_sem):
        def send(i, carry):
            peer = lax.rem(me + i, devices)
            pltpu.make_async_remote_copy(
                src_ref=src_of(peer),
                dst_ref=dst,
                send_sem=send_sem,
                recv_sem=recv_sem,
                device_id=(peer // npy, lax.rem(peer, npy)),
                device_id_type=MESH,
            ).start()
            return carry

        lax.fori_loop(1, devices, send, 0)

    def await_all(ref, size, sem):
        part = ref.at[pl.ds(0, size * (devices - 1))]
        pltpu.make_async_copy(part, part, sem).wait()

    def start_exchange(layer):
        h = h_ref[...]
        picked = dot(onehot(pidx_ref[...], (halo + cslots, cells), 1), h).astype(BF)
        send_buf[layer] = picked
        source[layer, pl.ds(0, cells)] = h
        coarse[layer, place(me, cslots)] = picked[halo:]
        copies = []
        for j, target in enumerate(targets):
            copy = pltpu.make_async_remote_copy(
                src_ref=send_buf.at[layer, pl.ds(offsets[j], sizes[j])],
                dst_ref=source.at[layer, pl.ds(cells + offsets[j], sizes[j])],
                send_sem=halo_send.at[layer, j],
                recv_sem=halo_recv.at[layer, j],
                device_id=target,
                device_id_type=MESH,
            )
            copy.start()
            copies.append(copy)
        to_all(
            lambda peer: send_buf.at[layer, pl.ds(halo, cslots)],
            coarse.at[layer, place(me, cslots)],
            coarse_send.at[layer],
            coarse_recv.at[layer],
        )
        return copies

    h_ref[...] = lat_ref[...]
    copies = start_exchange(0)
    placing = onehot(place_ref[...], (devices * block, long_ref.shape[0]), 0)
    tags = jnp.broadcast_to(cols_ref[:, 2:3].astype(F32), (long_ref.shape[0], 128)).astype(BF)
    labels_out[...] = dot(placing, tags).astype(BF)
    labels_in[place(me, block)] = labels_out[place(me, block)]
    to_all(
        lambda peer: labels_out.at[place(peer, block)],
        labels_in.at[place(me, block)],
        label_send.at[0],
        label_recv.at[0],
    )

    group = 16

    def regroup(i, carry):
        base = pl.multiple_of(i * group, group)
        taken = fine_ref[pl.ds(base, group)].astype(F32)
        for q in range(features // 128):
            lanes = slice(128 * q, 128 * q + 128)
            for j in range(group):
                spread_ref[q, pl.ds(8 * j, degree), :] = taken[j][:, lanes]
        for k in range(degree):
            for q in range(features // 128):
                lanes = slice(128 * q, 128 * q + 128)
                fine_out[k, pl.ds(base, group), lanes] = spread_ref.at[q][
                    pl.ds(k, group, stride=8), :
                ].astype(BF)
        return carry

    lax.fori_loop(0, cells // group, regroup, 0)
    for k in range(degree):
        onehots[k] = onehot(sidx_ref[:, k : k + 1], (cells, cells + halo), 1)
    long_out[...] = long_ref[...]

    for layer in range(layers):
        for j in range(4):
            loads[4 * layer + j].wait()
        if layer > 0:
            copies = start_exchange(layer)
        edge_part = ei.at[layer, pl.ds(0, features)]
        send_part = ei.at[layer, pl.ds(features, features)]
        receive_part = ei.at[layer, pl.ds(2 * features, features)]
        gains = eg_ref[layer : layer + 1, :]
        recv_terms[...] = dot(h_ref[...], receive_part[...])
        incoming[...] = jnp.zeros_like(incoming)
        for copy in copies:
            copy.wait()
        terms = dot(source[layer], send_part[...]).astype(BF)
        source[layer] = terms

        def fine(k, carry):
            before = fine_out[k]
            inner = dot(before, edge_part[...]) + dot(onehots[k], source[layer]) + recv_terms[...]
            after = finish(before, inner, eo[layer], gains)
            fine_out[k] = after
            incoming[...] += after.astype(F32)
            return carry

        lax.fori_loop(0, degree // 2, fine, 0)

        await_all(coarse.at[layer], cslots, coarse_recv.at[layer])
        table = coarse[layer]
        long_count = long_ref.shape[0]
        wide = (long_count, devices * cslots)
        from_rows = dot(onehot(cols_ref[:, 0:1], wide, 1), table).astype(BF)
        to_rows = dot(onehot(cols_ref[:, 1:2], wide, 1), table).astype(BF)
        before = long_out[...]
        inner = dot(before, edge_part[...])
        inner = inner + dot(from_rows, send_part[...])
        inner = inner + dot(to_rows, receive_part[...])
        after = finish(before, inner, eo[layer], gains)
        long_out[...] = after
        bucket[layer] = dot(
            onehot(place_ref[...], (devices * block, long_count), 0), after
        ).astype(BF)
        arrived[layer, place(me, block)] = bucket[layer, place(me, block)]
        to_all(
            lambda peer: bucket.at[layer, place(peer, block)],
            arrived.at[layer, place(me, block)],
            bucket_send.at[layer],
            bucket_recv.at[layer],
        )

        lax.fori_loop(degree // 2, degree, fine, 0)

        if layer == 0:
            await_all(labels_in, block, label_recv.at[0])
            names = labels_in[:, 0:1].astype(F32)
            lane = lax.broadcasted_iota(jnp.int32, (devices * block, cslots), 1).astype(F32)
            chooser = jnp.where(lane + 1.0 == names, 1.0, 0.0).astype(BF)
            owner = onehot(slots_ref[...], (cells, cslots), 0)
            select_ref[...] = lax.dot_general(
                owner, chooser, (((1,), (1,)), ((), ())), preferred_element_type=F32
            ).astype(BF)
        h = h_ref[...]
        inner = dot(h, ni[layer, pl.ds(0, features)])
        await_all(arrived.at[layer], block, bucket_recv.at[layer])
        total = (incoming[...] + dot(select_ref[...], arrived[layer])).astype(BF)
        inner = inner + dot(total, ni[layer, pl.ds(features, features)])
        h_ref[...] = finish(h, inner, no[layer], ng_ref[layer : layer + 1, :])

    nodes_out[...] = h_ref[...]
    await_all(labels_out, block, label_send.at[0])
    for layer in range(layers):
        await_all(coarse.at[layer], cslots, coarse_send.at[layer])
        await_all(bucket.at[layer], block, bucket_send.at[layer])


def sender_slots(neighbours, rows, columns):
    cells, degree = rows * columns, neighbours.shape[-1]
    code = neighbours + (neighbours >= 4).astype(jnp.int32)
    r = lax.broadcasted_iota(jnp.int32, neighbours.shape, 0) + code // 3 - 1
    c = lax.broadcasted_iota(jnp.int32, neighbours.shape, 1) + code % 3 - 1
    wr, hr = up16(columns), up16(rows)
    corner = cells + 2 * wr + 2 * hr
    top, bottom, west, east = r < 0, r >= rows, c < 0, c >= columns
    middle = jnp.where(west, cells + 2 * wr + r, jnp.where(east, cells + 2 * wr + hr + r, r * columns + c))
    above = jnp.where(west, corner, jnp.where(east, corner + 16, cells + c))
    below = jnp.where(west, corner + 32, jnp.where(east, corner + 48, cells + wr + c))
    return jnp.where(top, above, jnp.where(bottom, below, middle)).reshape(cells, degree)


def shards(
    counts,
    node_latents, fine_edges, long_edges, neighbours, coarse_slots, long_senders, long_receivers,
    edge_inner, edge_outer, edge_gain, node_inner, node_outer, node_gain,
):
    rows, columns, features = node_latents.shape
    degree = fine_edges.shape[2]
    hidden = edge_inner.shape[2]
    coarse_count = coarse_slots.shape[0]
    long_count = long_edges.shape[0]
    layers = edge_inner.shape[0]
    devices = counts[0] * counts[1]
    cells = rows * columns
    capacity = (2 * long_count + devices - 1) // devices
    block = up16(capacity)
    cslots = up16(coarse_count)

    wr, hr = up16(columns), up16(rows)
    cell = np.arange(cells).reshape(rows, columns)
    fixed = []
    for part, size in (
        (cell[-1], wr), (cell[0], wr), (cell[:, -1], hr), (cell[:, 0], hr),
        (cell[-1:, -1], 16), (cell[-1:, 0], 16), (cell[:1, -1], 16), (cell[:1, 0], 16),
    ):
        fixed.append(np.concatenate([part, np.full(size - len(part), -1)]))
    fixed = np.concatenate(fixed).astype(np.int32)
    halo = len(fixed)
    padded_slots = jnp.pad(coarse_slots, (0, cslots - coarse_count), constant_values=-1)
    pidx = jnp.concatenate([jnp.asarray(fixed), padded_slots])[:, None]

    owners = long_receivers // coarse_count
    within = long_receivers - owners * coarse_count
    earlier = lax.broadcasted_iota(jnp.int32, (long_count, long_count), 0) < lax.broadcasted_iota(
        jnp.int32, (long_count, long_count), 1
    )
    ranking = jnp.sum(
        ((owners[:, None] == owners[None, :]) & earlier).astype(jnp.int32), axis=0
    )
    placed = (owners * block + ranking)[None, :]
    from_owner = long_senders // coarse_count
    cols = jnp.stack(
        [
            from_owner * cslots + (long_senders - from_owner * coarse_count),
            owners * cslots + within,
            within + 1,
        ],
        axis=1,
    )
    vmem = pl.BlockSpec(memory_space=pltpu.VMEM)
    hbm = pl.BlockSpec(memory_space=pltpu.HBM)
    dma = pltpu.SemaphoreType.DMA
    nodes, fine, long_rows = pl.pallas_call(
        functools.partial(kernel, rows, columns, counts, block),
        out_shape=(
            jax.ShapeDtypeStruct((cells, features), BF),
            jax.ShapeDtypeStruct((degree, cells, features), BF),
            jax.ShapeDtypeStruct((long_count, features), BF),
        ),
        in_specs=[vmem] * 10 + [hbm] * 4,
        out_specs=(vmem, vmem, vmem),
        scratch_shapes=[
            pltpu.VMEM((cells, features), BF),
            pltpu.VMEM((degree, cells, cells + halo), BF),
            pltpu.VMEM((features // 128, 128, 128), F32),
            pltpu.VMEM((cells, hidden), F32),
            pltpu.VMEM((cells, features), F32),
            pltpu.VMEM((cells, devices * block), BF),
            pltpu.VMEM((layers, halo + cslots, features), BF),
            pltpu.VMEM((layers, cells + halo, features), BF),
            pltpu.VMEM((layers, devices * cslots, features), BF),
            pltpu.VMEM((layers, devices * block, features), BF),
            pltpu.VMEM((layers, devices * block, features), BF),
            pltpu.VMEM((devices * block, 128), BF),
            pltpu.VMEM((devices * block, 128), BF),
            pltpu.VMEM(edge_inner.shape, BF),
            pltpu.VMEM(edge_outer.shape, BF),
            pltpu.VMEM(node_inner.shape, BF),
            pltpu.VMEM(node_outer.shape, BF),
            dma((layers, 4)),
            dma((layers, 8)),
            dma((layers, 8)),
            dma((layers,)),
            dma((layers,)),
            dma((layers,)),
            dma((layers,)),
            dma((1,)),
            dma((1,)),
        ],
        compiler_params=pltpu.CompilerParams(
            has_side_effects=True, vmem_limit_bytes=62 * 1024 * 1024
        ),
    )(
        node_latents.reshape(cells, features),
        fine_edges.reshape(cells, degree, features),
        long_edges,
        sender_slots(neighbours, rows, columns),
        pidx,
        cols,
        placed,
        padded_slots[None, :],
        edge_gain,
        node_gain,
        edge_inner,
        edge_outer,
        node_inner,
        node_outer,
    )
    return (
        nodes.reshape(node_latents.shape),
        jnp.transpose(fine, (1, 0, 2)).reshape(fine_edges.shape),
        long_rows,
    )


def solution(mesh):
    in_specs = (
        P("px", "py", None),
        P("px", "py", None, None),
        P(("px", "py"), None),
        P("px", "py", None),
        P(("px", "py")),
        P(("px", "py")),
        P(("px", "py")),
        P(),
        P(),
        P(),
        P(),
        P(),
        P(),
    )
    out_specs = (P("px", "py", None), P("px", "py", None, None), P(("px", "py"), None))
    counts = (mesh.shape["px"], mesh.shape["py"])
    return jax.shard_map(
        functools.partial(shards, counts),
        mesh=mesh,
        in_specs=in_specs,
        out_specs=out_specs,
        check_vma=False,
    )
```

time: 338 us -> 119 us (0.35)
  blocking collectives: 155 us -> 0 us
  Pallas kernels: 0 us -> 98.2 us
  local copies, waits for them, and re-layouts: 74.5 us -> 15.1 us
  matrix products: 44.2 us -> 0 us
  other arithmetic: 37.5 us -> 4.54 us
  starting transfers between devices: 23 us -> 0 us
    all_gather x2 -> x0, blocking collectives: 155 us -> none  [shards(): coarse = lax.all_gather(own_coarse, ('px', 'py'), axis=0, tiled=True)]
    pallas_call x0 -> x1, Pallas kernels: none -> 98.2 us  [shards(): pl.pallas_call(functools.partial(kernel, rows, columns, counts, block), o...]
    dot_general x18 -> x0, matrix products: 44.2 us -> none  [the longest x6 25 us: finish(): output = jnp.dot(hidden, outer, preferred_element_type=jnp.float32)]
    gather x8 -> x0, local copies, waits for them, and re-layouts: 19.2 us -> none  [the longest x2 12.6 us: shards(): jnp.take(sender_terms, sender_index, axis=0)]
    add x5 -> x0, local copies, waits for them, and re-layouts: 18.6 us -> none  [the longest x4 18.4 us: shards(): inner_sum.reshape(patch_cells, degree, -1) + receiver_terms[:, None, :]]
    reduce_sum x9 -> x1, other arithmetic: 16.9 us -> 0.1 us  [shards(): jnp.sum(((owners[:, None] == owners[None, :]) & earlier).astype(jnp.int32...]
    all_to_all x3 -> x0, starting transfers between devices: 12.9 us -> none  [the longest x2 6.84 us: owner_sums(): lax.all_to_all(bucket.reshape(devices, capacity, features), ('px', 'py'),...]
    ppermute x8 -> x0, starting transfers between devices: 10.1 us -> none  [the longest x4 6.07 us: with_halo(): lax.ppermute(head, axis, [((i + 1) % count, i) for i in range(count)])]
  transfers between devices with their start and end apart: 11 -> 0, of which waited for: 0 -> 0; matrix products, arithmetic and copies ran while one was open for 38% -> 0% of each run, Pallas kernels for 0% -> 0%
where the time goes in v1:
time: 119 us
  Pallas kernels  98.2 us (83%)
  local copies, waits for them, and re-layouts  15.1 us (13%)
  other arithmetic  4.54 us (4%)
    pallas_call x1, Pallas kernels, shards(): pl.pallas_call(functools.partial(kernel, rows, columns, counts, block), o...  98.2 us
    unnamed x9, local copies, waits for them, and re-layouts  7.22 us
    reshape x1, local copies, waits for them, and re-layouts, shards(): jnp.transpose(fine, (1, 0, 2)).reshape(fine_edges.shape)  2.45 us

profile of v1, /device:TPU:0, one launch (start us, length us, event | category | flops | bytes accessed | tf_op | source)
XLA Modules:
  0.0 118.5 jit_solution(7489904676605884443)
XLA Ops:
  0.6 0.0 copy-start
  0.6 0.8 subtract_add_fusion
  1.5 1.2 %pad_bitcast_fusion = (s32[1,32]{1,0:T(1,128)}, s32[32]{0:T(128)S(1)}) fusion(s32[20]{0:T(128)} %param.18), kind=kLoop, calls=%fused_computation.24 | loop fusion | bytes 336 | tf_op jit(solution)/shard_map/broadcast_in_dim | solution.py:344
  2.7 0.8 pad_add_fusion.1
  3.4 0.7 multiply_add_fusion.1
  4.1 0.1 convert_reduce_fusion
  4.2 1.3 %multiply_add_fusion = (s32[160]{0:T(256)}, s32[160]{0:T(256)S(1)}) fusion(s32[160]{0:T(256)S(1)} %convert_reduce_fusion, s32[160]{0:T(256)S(1)} %get-tuple-element.22, s32[160]{0:T(256)} %param.20), kind=kLoop, calls=%fused_computation.19 | loop fusion | flops 800 | bytes 3200 | tf_op jit(solution)/shard_map/add | solution.py:283
  5.5 0.9 select_select_fusion
  6.4 0.1 reshape.25
  6.5 0.8 copy.42.cols_ref
  7.2 0.8 copy.41.pidx_ref
  8.0 0.8 copy.40.sidx_ref
  8.8 1.2 copy.38
  10.0 0.8 reshape.23.lat_ref
  10.8 0.0 copy-done
  10.8 2.6 %copy.39 = bf16[16,20,6,512]{3,2,1,0:T(8,128)(2,1)} copy(bf16[16,20,6,512]{3,0,2,1:T(8,128)(2,1)S(1)} %copy-done) | data formatting | bytes 3932160 | tf_op args[1]
  13.4 98.2 %shard_map.157 = (bf16[320,512]{1,0:T(8,128)(2,1)}, bf16[6,320,512]{2,1,0:T(8,128)(2,1)}, bf16[160,512]{1,0:T(8,128)(2,1)}) custom-call(bf16[320,512]{1,0:T(8,128)(2,1)} %reshape.23.lat_ref, bf16[320,6,512]{2,1,0:T(8,128)(2,1)} %bitcast.13, bf16[160,512]{1,0:T(8,128)(2,1)} %long_ref.1, s32[320,6]{1,0:T(8,128)} %copy.40.sidx_ref, s32[192,1]{1,0:T(8,128)} %copy.41.pidx_ref, ...), custom_call_target="tpu_custom_call" | custom-call | tf_op jit(solution)/shard_map/pallas_call | solution.py:296
  111.6 1.0 reshape.26
  112.6 0.8 copy.43
  113.5 2.5 %reshape.27 = bf16[16,20,6,512]{3,1,0,2:T(8,128)(2,1)S(1)} reshape(bf16[320,6,512]{2,0,1:T(8,128)(2,1)} %bitcast.14) | data formatting | bytes 3932160 | tf_op jit(solution)/shard_map/reshape | solution.py:354
  115.9 0.0 copy-start.1
  115.9 1.9 %copy.44 = bf16[16,20,6,512]{3,0,2,1:T(8,128)(2,1)} copy(bf16[16,20,6,512]{3,1,0,2:T(8,128)(2,1)S(1)} %reshape.27) | data formatting | bytes 3932160
  117.9 0.0 copy-done.1
  117.9 0.7 copy.46
  (1 shorter events, 0.0 us)
Async XLA Ops:
  0.6 10.1 %copy-start = (bf16[16,20,6,512]{3,0,2,1:T(8,128)(2,1)S(1)}, bf16[16,20,6,512]{3,0,2,1:T(8,128)(2,1)}, u32[]{:S(2)}) copy-start(bf16[16,20,6,512]{3,0,2,1:T(8,128)(2,1)} %param.15) | copy-start | bytes 5898244
  115.9 1.9 %copy-start.1 = (bf16[160,512]{1,0:T(8,128)(2,1)S(1)}, bf16[160,512]{1,0:T(8,128)(2,1)}, u32[]{:S(2)}) copy-start(bf16[160,512]{1,0:T(8,128)(2,1)} %get-tuple-element.32) | copy-start | bytes 491524
